TPU v7x, 32 devices: a whole 2x2x4 slice. The times are simulated.
32 devices in a mesh: layer: 4 (over x, core), lat: 8 (over z, y).
Axes of the slice: x: 2, y: 2, z: 4, core: 2. Of those that a mesh axis runs over, the one named last changes fastest.
Arguments:
- resid_in: bfloat16 [4, 4096, 256], P('layer', 'lat'), may hold values from -6 to 6
- resid_out: bfloat16 [4, 4096, 256], P('layer', 'lat'), may hold values from -80 to 80
- token_ids: int32 [256], replicated, may hold values from 0 to 128255, as said below
- active_mask: int32 [4, 6144, 256], P('layer', 'lat'), may hold values 0 or 1
- enc_weight: bfloat16 [4, 6144, 4096], P('layer', 'lat'), may hold values from -0.09375 to 0.09375
- enc_bias: bfloat16 [4, 6144], P('layer', 'lat'), may hold values from -3 to 3
- dec_weight: bfloat16 [4, 4, 6144, 4096], P('layer', None, 'lat'), may hold values from -0.078125 to 0.078125
- dec_bias: bfloat16 [4, 4096], P('layer', 'lat'), may hold values from -3 to 3
Outputs:
- enc_grad: bfloat16 [4, 6144, 4096], P('layer', 'lat')
- dec_grad: bfloat16 [4, 4, 6144, 4096], P('layer', None, 'lat')
- total_loss: float32 [], replicated
Inputs may be any that keep to these rules, and one draw needn't show every extreme that they name: `token_ids`: ids of the Llama 3 vocabulary; the begin-of-text id 128000 stands at position 0 and at scattered other positions.
All inputs are finite; a program needn't handle non-finite values. No bound on the sum of `active_mask` on one device may be relied on, other than what follows from the above.
Results may differ from a plain program's by a relative error of at most 0.007.
Values may be sent and summed in bfloat16 or wider, within the bound.
A program may use at most 128 MiB of HBM per device.

v0:
```python
import jax
import jax.numpy as jnp
from jax import lax
from jax.sharding import PartitionSpec as P

EPSILON = 1e-05


def on_device(
    resid_in, resid_out, token_ids, active_mask, enc_weight, enc_bias, dec_weight, dec_bias
):
    layer_count = lax.axis_size("layer")
    layer_here = lax.axis_index("layer")
    inputs_local = resid_in[0]
    weight_enc = enc_weight[0]
    lat_rows = weight_enc.shape[0]
    feature_count = weight_enc.shape[1]
    token_count = inputs_local.shape[1]
    whole_inputs = lax.all_gather(inputs_local, "lat", axis=0, tiled=True)
    preact = jnp.dot(weight_enc, whole_inputs, preferred_element_type=jnp.float32)
    preact = preact + enc_bias[0].astype(jnp.float32)[:, None]
    gating = active_mask[0].astype(jnp.float32)
    latents = (gating * preact).astype(jnp.bfloat16)
    source_ids = jnp.arange(layer_count)
    gathered = lax.all_gather(latents[None], "layer", axis=0, tiled=True)
    acts_stack = jnp.where(
        (source_ids <= layer_here)[:, None, None], gathered, jnp.zeros((), jnp.bfloat16)
    )
    stack_rows = acts_stack.reshape(layer_count * lat_rows, token_count)
    weight_rows = dec_weight[0].reshape(layer_count * lat_rows, feature_count)
    kept_tokens = (token_ids != 128000).astype(jnp.float32)
    total_cells = feature_count * token_count
    wanted = resid_out[0].astype(jnp.float32)
    recon = lax.psum_scatter(
        lax.dot_general(
            weight_rows, stack_rows, (((0,), (0,)), ((), ())), preferred_element_type=jnp.float32
        ),
        "lat",
        scatter_dimension=0,
        tiled=True,
    )
    recon = recon + dec_bias[0].astype(jnp.float32)[:, None]
    centered = wanted - jnp.mean(wanted, axis=1, keepdims=True)
    residual_err = kept_tokens[None, :] * (recon - wanted)
    squares_err, squares_tgt = lax.psum(
        (jnp.sum(residual_err * residual_err), jnp.sum(centered * centered)), "lat"
    )
    spread = squares_tgt / total_cells + EPSILON
    layer_loss = squares_err / (2.0 * spread * total_cells)
    total_loss = lax.psum(layer_loss, "layer")
    out_grad = (residual_err / spread).astype(jnp.bfloat16)
    full_grad = lax.all_gather(out_grad, "lat", axis=0, tiled=True)
    grad_rows = jnp.dot(weight_rows, full_grad, preferred_element_type=jnp.float32).reshape(
        layer_count, lat_rows, token_count
    )
    grad_rows = grad_rows * (source_ids <= layer_here).astype(jnp.float32)[:, None, None]
    dec_out = lax.dot_general(
        stack_rows, full_grad, (((1,), (1,)), ((), ())), preferred_element_type=jnp.float32
    )
    dec_out = dec_out.astype(jnp.bfloat16).reshape(1, layer_count, lat_rows, feature_count)
    latent_grad = lax.psum_scatter(grad_rows, "layer", scatter_dimension=0, tiled=True)[0]
    preact_grad = (gating * latent_grad).astype(jnp.bfloat16)
    enc_out = lax.dot_general(
        preact_grad, whole_inputs, (((1,), (1,)), ((), ())), preferred_element_type=jnp.float32
    )
    return (enc_out.astype(jnp.bfloat16)[None], dec_out, total_loss)


def solution(mesh):
    in_specs = (
        P("layer", "lat", None),
        P("layer", "lat", None),
        P(),
        P("layer", "lat", None),
        P("layer", "lat", None),
        P("layer", "lat"),
        P("layer", None, "lat", None),
        P("layer", "lat"),
    )
    out_specs = (P("layer", "lat", None), P("layer", None, "lat", None), P())
    return jax.shard_map(
        on_device, mesh=mesh, in_specs=in_specs, out_specs=out_specs, check_vma=False
    )
```

profile of v0, /device:TPU:0, one launch (start us, length us, event | category | flops | bytes accessed | tf_op | source)
XLA Modules:
  0.0 334.2 jit_solution(15536479008416231452)
XLA Ops:
  7.2 0.0 all-gather.8.cloned.1.call-start
  7.2 0.7 all-gather.8.cloned.1.call-update
  7.9 0.0 all-gather.10.cloned.1.call-start
  7.9 0.7 convert_reduce_fusion.1
  8.6 53.5 %all-gather.8.cloned.1.call-done = bf16[1,4096,256]{2,1,0:T(8,128)(2,1)} async-done(((bf16[1,512,256]{2,1,0:T(8,128)(2,1)}), bf16[1,4096,256]{2,1,0:T(8,128)(2,1)}) %all-gather.8.cloned.1.call-update) | async-done | bytes 2097168 | tf_op jit(solution)/shard_map/all_gather | solution.py:19
  62.2 6.1 %fusion.15 = bf16[768,256]{1,0:T(8,128)(2,1)} fusion(bf16[1,4096,256]{2,1,0:T(8,128)(2,1)} %all-gather.8.cloned.1.call-done, bf16[1,768,4096]{2,1,0:T(8,128)(2,1)} %param.12, s32[1,768,256]{2,1,0:T(8,128)} %param.11, f32[768]{0:T(1024)S(1)} %convert_reduce_fusion.1), kind=kOutput, calls=%fused_computation.13 | convolution fusion | flops 1611399168 | bytes 9571328 | tf_op jit(solution)/shard_map/dot_general | solution.py:20
  68.2 0.0 all-gather.10.cloned.1.call-update
  68.3 0.0 reduce-scatter.3.cloned.1.call-start
  68.3 18.2 %all-gather.10.cloned.1.call-done = bf16[3072,256]{1,0:T(8,128)(2,1)} async-done(((bf16[768,256]{1,0:T(8,128)(2,1)}), bf16[3072,256]{1,0:T(8,128)(2,1)}) %all-gather.10.cloned.1.call-update) | async-done | bytes 1572880 | tf_op jit(solution)/shard_map/all_gather | solution.py:25
  86.6 1.6 broadcast_select_fusion
  88.2 13.7 %convolution_bitcast_fusion = f32[4096,256]{0,1:T(8,128)} fusion(bf16[3072,256]{1,0:T(8,128)(2,1)S(1)} %bitcast.66, bf16[3072,4096]{1,0:T(8,128)(2,1)} %bitcast.64), kind=kOutput, calls=%fused_computation.5 | convolution fusion | flops 6442450944 | bytes 30932992 | tf_op jit(solution)/shard_map/dot_general | solution.py:35
  101.8 0.0 reduce-scatter.3.cloned.1.call-update
  101.8 0.0 all-gather.6.cloned.1.call-start
  101.9 0.9 copy-done.1
  102.8 0.1 copy.11
  102.9 0.0 copy-done.2
  102.9 0.1 convert_reduce_fusion
  103.0 87.4 %reduce-scatter.3.cloned.1.call-done = f32[512,256]{0,1:T(8,128)} async-done(((f32[4096,256]{0,1:T(8,128)}), f32[512,256]{0,1:T(8,128)}) %reduce-scatter.3.cloned.1.call-update) | async-done | bytes 524304 | tf_op jit(solution)/shard_map/reduce_scatter | solution.py:34
  190.5 1.9 multiply_reduce_fusion
  192.4 20.8 %all-reduce = (f32[]{:T(128)}, f32[]{:T(128)}) all-reduce(f32[]{:T(128)} %get-tuple-element.4, f32[]{:T(128)} %get-tuple-element.3), channel_id=1, replica_groups=mesh['layer'=4,'lat'=8] {'lat'}, use_global_device_ids=true, to_apply=%region_3.4 | all-reduce | flops 2 | bytes 16 | tf_op jit(solution)/shard_map/psum | solution.py:45
  213.8 1.9 divide_convert_fusion
  215.7 0.0 all-gather.6.cloned.1.call-update
  215.7 0.0 reduce-scatter.5.cloned.1.call-start
  215.8 48.4 %all-gather.6.cloned.1.call-done = bf16[4096,256]{0,1:T(8,128)(2,1)} async-done(((bf16[512,256]{0,1:T(8,128)(2,1)}), bf16[4096,256]{0,1:T(8,128)(2,1)}) %all-gather.6.cloned.1.call-update) | async-done | bytes 2097168 | tf_op jit(solution)/shard_map/all_gather | solution.py:52
  264.2 13.3 %convolution_bitcast_fusion.1 = f32[3072,256]{0,1:T(8,128)} fusion(bf16[4096,256]{0,1:T(8,128)(2,1)} %all-gather.6.cloned.1.call-done, bf16[3072,4096]{1,0:T(8,128)(2,1)} %bitcast.65), kind=kOutput, calls=%fused_computation.6 | convolution fusion | flops 6442450944 | bytes 30408704 | tf_op jit(solution)/shard_map/dot_general | solution.py:53
  277.5 3.5 %copy.12 = f32[3072,256]{1,0:T(8,128)} copy(f32[3072,256]{0,1:T(8,128)} %convolution_bitcast_fusion.1) | data formatting | bytes 6291456 | tf_op jit(solution)/shard_map/dot_general | solution.py:53
  281.1 3.9 %broadcast_multiply_fusion = f32[4,768,256]{2,1,0:T(8,128)} fusion(f32[4,768,256]{2,1,0:T(8,128)} %bitcast.68, f32[4]{0:T(128)S(1)} %fusion.27), kind=kLoop, calls=%fused_computation.9 | loop fusion | flops 786432 | bytes 6291472 | tf_op jit(solution)/shard_map/mul | solution.py:56
  285.0 0.0 reduce-scatter.5.cloned.1.call-update
  285.7 6.8 %psum.23 = f32[]{:T(128)} all-reduce(f32[]{:T(128)S(6)} %div.23), channel_id=1, replica_groups=mesh['layer'=4,'lat'=8] {'layer'}, use_global_device_ids=true, to_apply=%region_7.8 | all-reduce | flops 1 | bytes 8 | tf_op jit(solution)/shard_map/psum | solution.py:50
  292.5 14.1 %convolution_convert_fusion = bf16[3072,4096]{1,0:T(8,128)(2,1)} fusion(bf16[3072,256]{1,0:T(8,128)(2,1)S(1)} %bitcast.67, bf16[4096,256]{0,1:T(8,128)(2,1)} %all-gather.6.cloned.1.call-done), kind=kOutput, calls=%fused_computation | convolution fusion | flops 6455033856 | bytes 28835840 | tf_op jit(solution)/shard_map/dot_general | solution.py:57
  306.6 14.6 %reduce-scatter.5.cloned.1.call-done = f32[1,768,256]{2,1,0:T(8,128)} async-done(((f32[4,768,256]{2,1,0:T(8,128)}), f32[1,768,256]{2,1,0:T(8,128)}) %reduce-scatter.5.cloned.1.call-update) | async-done | bytes 786448 | tf_op jit(solution)/shard_map/reduce_scatter | solution.py:61
  321.3 6.4 %fusion.2 = bf16[1,768,4096]{2,1,0:T(8,128)(2,1)} fusion(bf16[1,4096,256]{2,1,0:T(8,128)(2,1)} %all-gather.8.cloned.1.call-done, f32[1,768,256]{2,1,0:T(8,128)} %reduce-scatter.5.cloned.1.call-done, s32[1,768,256]{2,1,0:T(8,128)S(1)} %copy-done), kind=kOutput, calls=%fused_computation.4 | convolution fusion | flops 1614348288 | bytes 9961472 | tf_op jit(solution)/shard_map/dot_general | solution.py:63
  (11 shorter events, 0.0 us)
Async XLA Ops:
  7.2 55.0 %all-gather.8.cloned.1.call-start = ((), (), s32[]{:S(2)}) async-start(), calls=%async_computation.5 | async-start | bytes 2359296 | tf_op jit(solution)/shard_map/all_gather | solution.py:19
  7.9 78.7 %all-gather.10.cloned.1.call-start = ((), (), s32[]{:S(2)}) async-start(), calls=%async_computation.6 | async-start | bytes 1966080 | tf_op jit(solution)/shard_map/all_gather | solution.py:25
  68.3 122.2 %reduce-scatter.3.cloned.1.call-start = ((), (), s32[]{:S(2)}) async-start(), calls=%async_computation.2 | async-start | bytes 4718592 | tf_op jit(solution)/shard_map/reduce_scatter | solution.py:34
  101.8 0.9 copy-start.1
  101.8 1.1 copy-start.2
  101.8 1.2 copy-start.3
  101.8 162.3 %all-gather.6.cloned.1.call-start = ((), (), s32[]{:S(2)}) async-start(), calls=%async_computation.3 | async-start | bytes 2359296 | tf_op jit(solution)/shard_map/all_gather | solution.py:52
  215.7 105.6 %reduce-scatter.5.cloned.1.call-start = ((), (), s32[]{:S(2)}) async-start(), calls=%async_computation.4 | async-start | bytes 3932160 | tf_op jit(solution)/shard_map/reduce_scatter | solution.py:61
  292.5 28.8 %copy-start = (s32[1,768,256]{2,1,0:T(8,128)S(1)}, s32[1,768,256]{2,1,0:T(8,128)}, u32[]{:S(2)}) copy-start(s32[1,768,256]{2,1,0:T(8,128)} %param.11) | copy-start | bytes 2359300
Sparse Core Ops, SparseCore 0:
  10.1 51.9 all-gather.7
  68.4 18.1 all-gather.9
  102.0 88.4 reduce-scatter.2
  215.8 48.3 all-gather.5
  285.1 36.1 reduce-scatter.4
where the time goes:
time: 335 us; the launch traced here: 334 us
  waiting for transfers between devices  223 us (67%)
  matrix products  53.6 us (16%)
  blocking collectives  27.6 us (8%)
  between operations  15.2 us (5%)
  other arithmetic  10 us (3%)
  local copies, waits for them, and re-layouts  4.56 us (1%)
    reduce_scatter x1, waiting for transfers between devices, on_device(): lax.psum_scatter(lax.dot_general(weight_rows, stack_rows, (((0,), (0,)),...  87.4 us
    all_gather x1, waiting for transfers between devices, on_device(): whole_inputs = lax.all_gather(inputs_local, 'lat', axis=0, tiled=True)  53.5 us
    all_gather x1, waiting for transfers between devices, on_device(): full_grad = lax.all_gather(out_grad, 'lat', axis=0, tiled=True)  48.4 us
    psum x1, blocking collectives, on_device(): lax.psum((jnp.sum(residual_err * residual_err), jnp.sum(centered * center...  20.8 us
    all_gather x1, waiting for transfers between devices, on_device(): gathered = lax.all_gather(latents[None], 'layer', axis=0, tiled=True)  18.2 us
    reduce_scatter x1, waiting for transfers between devices, on_device(): lax.psum_scatter(grad_rows, 'layer', scatter_dimension=0, tiled=True)[0]  14.6 us
    dot_general x1, matrix products, on_device(): lax.dot_general(stack_rows, full_grad, (((1,), (1,)), ((), ())), preferre...  14.1 us
    dot_general x1, matrix products, on_device(): lax.dot_general(weight_rows, stack_rows, (((0,), (0,)), ((), ())), prefer...  13.7 us
  transfers between devices with their start and end apart: 5, of which 5 were waited for; matrix products, arithmetic and copies ran while one was open for 5% of the time, Pallas kernels for 0%

commit v1 on v0

v1 whole, which is shorter than its diff:
```python
import functools

import jax
import jax.numpy as jnp
from jax import lax
from jax.experimental import pallas as pl
from jax.experimental.pallas import tpu as pltpu
from jax.sharding import PartitionSpec as P

EPSILON = 1e-05
F32 = jnp.float32
BF16 = jnp.bfloat16


class Place:
    def __init__(self, lat_count):
        self.me = lax.axis_index("lat")
        self.depth = lat_count // 2
        self.z = self.me // 2
        self.y = self.me % 2
        self.partner = self.me + 1 - 2 * self.y
        self.has_up = self.z < self.depth - 1
        self.has_down = self.z > 0


def send(src, dst, send_sem, recv_sem, lat):
    return pltpu.make_async_remote_copy(
        src_ref=src,
        dst_ref=dst,
        send_sem=send_sem,
        recv_sem=recv_sem,
        device_id={"lat": lat},
        device_id_type=pl.DeviceIdType.MESH,
    )


def greet(at):
    barrier = pltpu.get_barrier_semaphore()

    def hello(lat):
        pl.semaphore_signal(
            barrier, inc=1, device_id={"lat": lat}, device_id_type=pl.DeviceIdType.MESH
        )

    hello(at.partner)
    pl.when(at.has_up)(lambda: hello(at.me + 2))
    pl.when(at.has_down)(lambda: hello(at.me - 2))
    peers = 1 + at.has_up.astype(jnp.int32) + at.has_down.astype(jnp.int32)
    pl.semaphore_wait(barrier, peers)


class Gather:
    def __init__(self, at, own, whole, sems):
        self.at, self.own, self.whole, self.sems = at, own, whole, sems

    def hop(self, kind, d):
        at = self.at
        shard = at.me - 2 * d if kind in (0, 2) else at.me + 2 * d
        src = self.own if d == 0 else self.whole.at[shard]
        to = (at.me + 2, at.me - 2, at.partner, at.partner)[kind]
        later = d + 1 if kind < 2 else d
        return send(
            src, self.whole.at[shard], self.sems.at[0, kind, d], self.sems.at[1, kind, later], to
        )

    def landing(self, kind, d):
        at = self.at
        below = kind in (0, 2)
        shard = at.me - 2 * d if below else at.me + 2 * d
        if kind >= 2:
            shard = shard + 1 - 2 * at.y
        ref = self.whole.at[shard]
        return send(ref, ref, self.sems.at[0, kind, d], self.sems.at[1, kind, d], at.partner)

    def start(self):
        pl.when(self.at.has_up)(lambda: self.hop(0, 0).start())
        pl.when(self.at.has_down)(lambda: self.hop(1, 0).start())
        self.hop(2, 0).start()

    def step(self, d):
        at = self.at

        @pl.when(at.z >= d)
        def _():
            self.landing(0, d).wait_recv()
            pl.when(at.has_up)(lambda: self.hop(0, d).start())
            self.hop(2, d).start()

        @pl.when(at.z + d < at.depth)
        def _():
            self.landing(1, d).wait_recv()
            pl.when(at.has_down)(lambda: self.hop(1, d).start())
            self.hop(3, d).start()

    def finish(self):
        at = self.at
        for d in range(at.depth):

            @pl.when(at.z >= d)
            def _():
                self.landing(2, d).wait_recv()
                self.hop(2, d).wait_send()
                if d < at.depth - 1:
                    pl.when(at.has_up)(lambda: self.hop(0, d).wait_send())

            @pl.when(at.z + d < at.depth)
            def _():
                if d > 0:
                    self.landing(3, d).wait_recv()
                    self.hop(3, d).wait_send()
                if d < at.depth - 1:
                    pl.when(at.has_down)(lambda: self.hop(1, d).wait_send())


def gather_kernel(lat_count, own, wanted_ref, whole, stats, stat, big_sems, stat_sems, local_sem):
    at = Place(lat_count)
    greet(at)
    big = Gather(at, own, whole, big_sems)
    big.start()
    keep = pltpu.make_async_copy(own, whole.at[at.me], local_sem)
    keep.start()
    wanted = wanted_ref[...].astype(F32)
    centered = wanted - jnp.mean(wanted, axis=1, keepdims=True)
    total = jnp.sum(centered * centered, keepdims=True)
    stat[...] = jnp.broadcast_to(total, stat.shape)
    stats[at.me] = stat[...]
    small = Gather(at, stat, stats, stat_sems)
    small.start()
    for d in range(1, at.depth):
        big.step(d)
        small.step(d)
    keep.wait()
    big.finish()
    small.finish()


def reduce_kernel(
    lat_count,
    parts,
    wanted_ref,
    bias_ref,
    kept_ref,
    spread_ref,
    whole,
    stats,
    across_up,
    across_down,
    from_below,
    from_above,
    going_up,
    going_down,
    total,
    grad,
    stat,
    across_sems,
    line_sems,
    big_sems,
    stat_sems,
):
    at = Place(lat_count)
    depth = at.depth
    greet(at)

    def across(up, d):
        rung = at.z + d if up else at.z - d
        row = 0 if up else 1
        return send(
            parts.at[rung * 2 + 1 - at.y],
            (across_up if up else across_down).at[d],
            across_sems.at[0, row, d],
            across_sems.at[1, row, d],
            at.partner,
        )

    def along(up, d):
        row = 0 if up else 1
        return send(
            (going_up if up else going_down).at[d],
            (from_below if up else from_above).at[d - 1],
            line_sems.at[0, row, d],
            line_sems.at[1, row, d - 1],
            at.me + 2 if up else at.me - 2,
        )

    def arrived(up, d):
        row = 0 if up else 1
        ref = (from_below if up else from_above).at[d]
        send(ref, ref, line_sems.at[0, row, d], line_sems.at[1, row, d], at.partner).wait_recv()

    for d in range(depth - 1, -1, -1):
        pl.when(at.z + d < depth)(lambda: across(True, d).start())
        if d:
            pl.when(at.z >= d)(lambda: across(False, d).start())

    def forward(up, d):
        across(up, d).wait_recv()
        rung = at.z + d if up else at.z - d
        crossed = across_up if up else across_down
        came = from_below if up else from_above
        going = going_up if up else going_down
        behind = at.has_down if up else at.has_up
        mine = parts.at[rung * 2 + at.y]

        @pl.when(behind)
        def _():
            if d < depth - 1:
                arrived(up, d)
                going[d] = (
                    mine[...].astype(F32) + crossed[d].astype(F32) + came[d].astype(F32)
                ).astype(BF16)

        @pl.when(jnp.logical_not(behind))
        def _():
            going[d] = (mine[...].astype(F32) + crossed[d].astype(F32)).astype(BF16)

        along(up, d).start()

    for d in range(depth - 1, 0, -1):
        pl.when(at.z + d < depth)(lambda: forward(True, d))
        pl.when(at.z >= d)(lambda: forward(False, d))
    across(True, 0).wait_recv()
    total[...] = (
        parts[at.me].astype(F32)
        + across_up[0].astype(F32)
        + (bias_ref[...] - wanted_ref[...].astype(F32))
    )

    @pl.when(at.has_down)
    def _():
        arrived(True, 0)
        total[...] += from_below[0].astype(F32)

    @pl.when(at.has_up)
    def _():
        arrived(False, 0)
        total[...] += from_above[0].astype(F32)

    err = kept_ref[...] * total[...]
    grad[...] = (err / spread_ref[...]).astype(BF16)
    whole[at.me] = grad[...]
    big = Gather(at, grad, whole, big_sems)
    big.start()
    stat[...] = jnp.broadcast_to(jnp.sum(err * err, keepdims=True), stat.shape)
    stats[at.me] = stat[...]
    small = Gather(at, stat, stats, stat_sems)
    small.start()
    for d in range(1, depth):
        big.step(d)
        small.step(d)
    big.finish()
    small.finish()
    for d in range(depth - 1, -1, -1):

        @pl.when(at.z + d < depth)
        def _():
            across(True, d).wait_send()
            if d:
                along(True, d).wait_send()

        if d:

            @pl.when(at.z >= d)
            def _():
                across(False, d).wait_send()
                along(False, d).wait_send()


VMEM = pl.BlockSpec(memory_space=pltpu.VMEM)


def gather_inputs(inputs_local, wanted, lat_count):
    rows, tokens = inputs_local.shape
    depth = lat_count // 2
    return pl.pallas_call(
        functools.partial(gather_kernel, lat_count),
        out_shape=(
            jax.ShapeDtypeStruct((lat_count, rows, tokens), BF16),
            jax.ShapeDtypeStruct((lat_count, 8, 128), F32),
        ),
        in_specs=[VMEM] * 2,
        out_specs=(VMEM, VMEM),
        scratch_shapes=[
            pltpu.VMEM((8, 128), F32),
            pltpu.SemaphoreType.DMA((2, 4, depth + 1)),
            pltpu.SemaphoreType.DMA((2, 4, depth + 1)),
            pltpu.SemaphoreType.DMA,
        ],
        compiler_params=pltpu.CompilerParams(
            collective_id=0, has_side_effects=True, vmem_limit_bytes=32 << 20
        ),
    )(inputs_local, wanted)


def reduce_and_gather(parts, wanted, bias, kept, spread, lat_count):
    _, rows, tokens = parts.shape
    depth = lat_count // 2
    slots = pltpu.VMEM((depth, rows, tokens), BF16)
    return pl.pallas_call(
        functools.partial(reduce_kernel, lat_count),
        out_shape=(
            jax.ShapeDtypeStruct((lat_count, rows, tokens), BF16),
            jax.ShapeDtypeStruct((lat_count, 8, 128), F32),
        ),
        in_specs=[VMEM] * 5,
        out_specs=(VMEM, VMEM),
        scratch_shapes=[slots] * 6
        + [
            pltpu.VMEM((rows, tokens), F32),
            pltpu.VMEM((rows, tokens), BF16),
            pltpu.VMEM((8, 128), F32),
            pltpu.SemaphoreType.DMA((2, 2, depth)),
            pltpu.SemaphoreType.DMA((2, 2, depth)),
            pltpu.SemaphoreType.DMA((2, 4, depth + 1)),
            pltpu.SemaphoreType.DMA((2, 4, depth + 1)),
        ],
        compiler_params=pltpu.CompilerParams(
            collective_id=1, has_side_effects=True, vmem_limit_bytes=40 << 20
        ),
    )(parts, wanted, bias, kept, spread)


def on_device(
    resid_in, resid_out, token_ids, active_mask, enc_weight, enc_bias, dec_weight, dec_bias
):
    layer_count = lax.axis_size("layer")
    lat_count = lax.axis_size("lat")
    layer_here = lax.axis_index("layer")
    inputs_local = resid_in[0]
    wanted = resid_out[0]
    weight_enc = enc_weight[0]
    lat_rows = weight_enc.shape[0]
    feature_count = weight_enc.shape[1]
    feature_rows, token_count = inputs_local.shape
    total_cells = feature_count * token_count
    whole_inputs, target_stats = gather_inputs(inputs_local, wanted, lat_count)
    whole_inputs = whole_inputs.reshape(feature_count, token_count)
    spread = jnp.sum(target_stats[:, 0, 0]) / total_cells + EPSILON
    preact = jnp.dot(weight_enc, whole_inputs, preferred_element_type=F32)
    preact = preact + enc_bias[0].astype(F32)[:, None]
    gating = active_mask[0].astype(F32)
    latents = (gating * preact).astype(BF16)
    source_ids = jnp.arange(layer_count)
    gathered = lax.all_gather(latents[None], "layer", axis=0, tiled=True)
    acts_stack = jnp.where(
        (source_ids <= layer_here)[:, None, None], gathered, jnp.zeros((), BF16)
    )
    stack_rows = acts_stack.reshape(layer_count * lat_rows, token_count)
    weight_rows = dec_weight[0].reshape(layer_count * lat_rows, feature_count)
    kept_tokens = (token_ids != 128000).astype(F32)
    parts = lax.dot_general(
        weight_rows, stack_rows, (((0,), (0,)), ((), ())), preferred_element_type=F32
    ).astype(BF16)
    full_grad, err_stats = reduce_and_gather(
        parts.reshape(lat_count, feature_rows, token_count),
        wanted,
        dec_bias[0].astype(F32)[:, None],
        kept_tokens[None, :],
        jnp.broadcast_to(spread, (1, token_count)),
        lat_count,
    )
    full_grad = full_grad.reshape(feature_count, token_count)
    layer_loss = jnp.sum(err_stats[:, 0, 0]) / (2.0 * spread * total_cells)
    total_loss = lax.psum(layer_loss, "layer")
    grad_rows = jnp.dot(weight_rows, full_grad, preferred_element_type=F32).reshape(
        layer_count, lat_rows, token_count
    )
    grad_rows = (grad_rows * (source_ids <= layer_here).astype(F32)[:, None, None]).astype(BF16)
    dec_out = lax.dot_general(
        stack_rows, full_grad, (((1,), (1,)), ((), ())), preferred_element_type=F32
    )
    dec_out = dec_out.astype(BF16).reshape(1, layer_count, lat_rows, feature_count)
    latent_grad = lax.psum_scatter(grad_rows, "layer", scatter_dimension=0, tiled=True)[0]
    preact_grad = (gating * latent_grad.astype(F32)).astype(BF16)
    enc_out = lax.dot_general(
        preact_grad, whole_inputs, (((1,), (1,)), ((), ())), preferred_element_type=F32
    )
    return (enc_out.astype(BF16)[None], dec_out, total_loss)


def solution(mesh):
    in_specs = (
        P("layer", "lat", None),
        P("layer", "lat", None),
        P(),
        P("layer", "lat", None),
        P("layer", "lat", None),
        P("layer", "lat"),
        P("layer", None, "lat", None),
        P("layer", "lat"),
    )
    out_specs = (P("layer", "lat", None), P("layer", None, "lat", None), P())
    return jax.shard_map(
        on_device, mesh=mesh, in_specs=in_specs, out_specs=out_specs, check_vma=False
    )
```

time: 335 us -> 204 us (0.61)
  waiting for transfers between devices: 223 us -> 23.5 us
  Pallas kernels: 0 us -> 84.2 us
  blocking collectives: 27.6 us -> 6.4 us
  local copies, waits for them, and re-layouts: 4.56 us -> 18.9 us
  other arithmetic: 10 us -> 4.12 us
    all_gather x2 -> x0, waiting for transfers between devices: 102 us -> none  [the longest x1 53.5 us: on_device(): whole_inputs = lax.all_gather(inputs_local, 'lat', axis=0, tiled=True)]
    reduce_scatter x1 -> x0, waiting for transfers between devices: 87.4 us -> none  [on_device(): lax.psum_scatter(lax.dot_general(weight_rows, stack_rows, (((0,), (0,)),...]
    pallas_call x0 -> x2, Pallas kernels: none -> 84.2 us  [the longest x1 53.8 us: reduce_and_gather(): pl.pallas_call(functools.partial(reduce_kernel, lat_count), out_shape=(ja...]
    psum x1 -> x0, blocking collectives: 20.8 us -> none  [on_device(): lax.psum((jnp.sum(residual_err * residual_err), jnp.sum(centered * center...]
    reduce_scatter x1, waiting for transfers between devices: 14.6 us -> 6.68 us  [on_device(): lax.psum_scatter(grad_rows, 'layer', scatter_dimension=0, tiled=True)[0]]
    unnamed x9 -> x24, local copies, waits for them, and re-layouts: 1.02 us -> 7.39 us
    mul x1 -> x0, other arithmetic: 3.91 us -> none  [on_device(): grad_rows * (source_ids <= layer_here).astype(jnp.float32)[:, None, None]]
    convert_element_type x0 -> x2, local copies, waits for them, and re-layouts: none -> 3.45 us  [the longest x1 3.31 us: on_device(): parts = lax.dot_general(weight_rows, stack_rows, (((0,), (0,)), ((), ()))...]
  transfers between devices with their start and end apart: 5 -> 2, of which waited for: 5 -> 2; matrix products, arithmetic and copies ran while one was open for 5% -> 8% of each run, Pallas kernels for 0% -> 0%
where the time goes in v1:
time: 204 us
  Pallas kernels  84.2 us (41%)
  matrix products  50.9 us (25%)
  waiting for transfers between devices  23.5 us (12%)
  local copies, waits for them, and re-layouts  18.9 us (9%)
  between operations  15.6 us (8%)
  blocking collectives  6.4 us (3%)
  other arithmetic  4.12 us (2%)
    pallas_call x1, Pallas kernels, reduce_and_gather(): pl.pallas_call(functools.partial(reduce_kernel, lat_count), out_shape=(ja...  53.8 us
    pallas_call x1, Pallas kernels, gather_inputs(): pl.pallas_call(functools.partial(gather_kernel, lat_count), out_shape=(ja...  30.4 us
    all_gather x1, waiting for transfers between devices, on_device(): gathered = lax.all_gather(latents[None], 'layer', axis=0, tiled=True)  16.8 us
    dot_general x1, matrix products, on_device(): lax.dot_general(stack_rows, full_grad, (((1,), (1,)), ((), ())), preferre...  14.5 us
    dot_general x1, matrix products, on_device(): lax.dot_general(weight_rows, stack_rows, (((0,), (0,)), ((), ())), prefer...  13.2 us
    dot_general x1, matrix products, on_device(): jnp.dot(weight_rows, full_grad, preferred_element_type=F32)  12.2 us
    unnamed x24, local copies, waits for them, and re-layouts  7.39 us
    reduce_scatter x1, waiting for transfers between devices, on_device(): lax.psum_scatter(grad_rows, 'layer', scatter_dimension=0, tiled=True)[0]  6.68 us
  transfers between devices with their start and end apart: 2, of which 2 were waited for; matrix products, arithmetic and copies ran while one was open for 8% of the time, Pallas kernels for 0%

profile of v1, /device:TPU:0, one launch (start us, length us, event | category | flops | bytes accessed | tf_op | source)
XLA Modules:
  0.0 203.6 jit_solution(7502493140955914079)
XLA Ops:
  7.2 0.0 all-gather.3.cloned.1.call-start
  7.2 1.4 copy.13
  8.6 0.7 convert_reduce_fusion
  9.3 0.0 copy-start.3
  9.4 0.9 copy-done.3
  10.3 0.9 copy-done.5
  11.3 30.4 %shard_map.103 = (bf16[8,512,256]{2,1,0:T(8,128)(2,1)S(1)}, f32[8,8,128]{2,1,0:T(8,128)S(1)}) custom-call(bf16[512,256]{1,0:T(8,128)(2,1)S(1)} %bitcast.61, bf16[512,256]{1,0:T(8,128)(2,1)S(1)} %bitcast.59), custom_call_target="tpu_custom_call" | custom-call | tf_op jit(solution)/shard_map/pallas_call | solution.py:274
  41.7 1.3 copy-done
  43.0 5.4 %fusion.13 = bf16[768,256]{0,1:T(8,128)(2,1)} fusion(bf16[4096,256]{1,0:T(8,128)(2,1)S(1)} %bitcast.55, bf16[1,768,4096]{2,1,0:T(8,128)(2,1)} %param.12, s32[1,768,256]{1,2,0:T(8,128)S(1)} %copy.13, f32[768]{0:T(1024)S(1)} %convert_reduce_fusion), kind=kOutput, calls=%fused_computation.13 | convolution fusion | flops 1611399168 | bytes 9571328 | tf_op jit(solution)/shard_map/dot_general | solution.py:338
  48.4 0.0 all-gather.3.cloned.1.call-update
  48.4 0.0 reduce-scatter.2.cloned.1.call-start
  48.5 0.1 copy.15.bias_ref
  48.7 0.6 slice_reduce_fusion.1
  50.0 16.8 %all-gather.3.cloned.1.call-done = bf16[3072,256]{0,1:T(8,128)(2,1)} async-done(((bf16[768,256]{0,1:T(8,128)(2,1)}), bf16[3072,256]{0,1:T(8,128)(2,1)}) %all-gather.3.cloned.1.call-update) | async-done | bytes 1572880 | tf_op jit(solution)/shard_map/all_gather | solution.py:343
  66.8 3.3 %reshape.61 = bf16[4,768,256]{1,0,2:T(4,128)(2,1)S(1)} reshape(bf16[3072,256]{0,1:T(8,128)(2,1)} %all-gather.3.cloned.1.call-done) | data formatting | bytes 3145728 | tf_op jit(solution)/shard_map/all_gather | solution.py:343
  70.1 0.7 broadcast_select_fusion
  70.8 0.3 copy.18
  71.1 1.2 copy-done.6
  72.3 13.2 %fusion.3 = bf16[4096,256]{0,1:T(8,128)(2,1)} fusion(bf16[3072,256]{0,1:T(8,128)(2,1)S(1)} %bitcast.65, bf16[3072,4096]{1,0:T(8,128)(2,1)} %bitcast.68), kind=kOutput, calls=%fused_computation.6 | convolution fusion | flops 6443499520 | bytes 28835840 | tf_op jit(solution)/shard_map/dot_general | solution.py:350
  85.5 3.3 %copy.14 = bf16[4096,256]{1,0:T(8,128)(2,1)S(1)} copy(bf16[4096,256]{0,1:T(8,128)(2,1)} %fusion.3) | data formatting | bytes 4194304 | tf_op jit(solution)/shard_map/convert_element_type | solution.py:352
  88.8 53.8 %shard_map.104 = (bf16[8,512,256]{2,1,0:T(8,128)(2,1)S(1)}, f32[8,8,128]{2,1,0:T(8,128)S(1)}) custom-call(bf16[8,512,256]{2,1,0:T(8,128)(2,1)S(1)} %bitcast.54, bf16[512,256]{1,0:T(8,128)(2,1)S(1)} %bitcast.60, f32[512,1]{1,0:T(8,128)S(1)} %copy.15.bias_ref, f32[1,256]{1,0:T(1,128)S(1)} %bitcast.62, f32[1,256]{1,0:T(1,128)S(1)} %broadcast_in_dim.35.spread_ref), custom_call_target="tpu_custom_call" | custom-call | tf_op jit(solution)/shard_map/pallas_call | solution.py:298
  142.6 1.3 copy-done.2
  143.9 12.2 %convolution_bitcast_fusion = f32[3072,256]{0,1:T(8,128)S(1)} fusion(bf16[4096,256]{1,0:T(8,128)(2,1)} %bitcast.57, bf16[3072,4096]{1,0:T(8,128)(2,1)} %bitcast.69), kind=kOutput, calls=%fused_computation.7 | convolution fusion | flops 6442450944 | bytes 30408704 | tf_op jit(solution)/shard_map/dot_general | solution.py:364
  156.2 2.4 %copy.16 = f32[3072,256]{1,0:T(8,128)} copy(f32[3072,256]{0,1:T(8,128)S(1)} %convolution_bitcast_fusion) | data formatting | bytes 6291456 | tf_op jit(solution)/shard_map/dot_general | solution.py:364
  158.5 2.4 %copy.17 = f32[4,768,256]{1,2,0:T(8,128)S(1)} copy(f32[4,768,256]{2,1,0:T(8,128)} %bitcast.64) | data formatting | bytes 6291456 | tf_op jit(solution)/shard_map/reshape | solution.py:364
  160.9 1.4 multiply_convert_fusion
  162.4 0.0 reduce-scatter.2.cloned.1.call-update
  162.4 0.6 slice_reduce_fusion
  163.6 6.4 %psum.7 = f32[]{:T(128)} all-reduce(f32[]{:T(128)S(6)} %div.7), channel_id=1, replica_groups=mesh['layer'=4,'lat'=8] {'layer'}, use_global_device_ids=true, to_apply=%region_3.4 | all-reduce | flops 1 | bytes 8 | tf_op jit(solution)/shard_map/psum | solution.py:363
  170.1 14.5 %convolution_convert_fusion = bf16[3072,4096]{1,0:T(8,128)(2,1)} fusion(bf16[3072,256]{0,1:T(8,128)(2,1)} %bitcast.66, bf16[4096,256]{1,0:T(8,128)(2,1)} %bitcast.58), kind=kOutput, calls=%fused_computation | convolution fusion | flops 6455033856 | bytes 28835840 | tf_op jit(solution)/shard_map/dot_general | solution.py:368
  184.5 6.7 %reduce-scatter.2.cloned.1.call-done = bf16[1,768,256]{1,2,0:T(8,128)(2,1)} async-done(((bf16[4,768,256]{1,2,0:T(8,128)(2,1)}), bf16[1,768,256]{1,2,0:T(8,128)(2,1)}) %reduce-scatter.2.cloned.1.call-update) | async-done | bytes 393232 | tf_op jit(solution)/shard_map/reduce_scatter | solution.py:372
  191.2 5.6 %fusion.2 = bf16[1,768,4096]{2,1,0:T(8,128)(2,1)} fusion(bf16[4096,256]{1,0:T(8,128)(2,1)S(1)} %bitcast.56, bf16[1,768,256]{1,2,0:T(8,128)(2,1)} %reduce-scatter.2.cloned.1.call-done, s32[1,768,256]{1,2,0:T(8,128)S(1)} %copy-done.8), kind=kOutput, calls=%fused_computation.4 | convolution fusion | flops 1614544896 | bytes 9568256 | tf_op jit(solution)/shard_map/dot_general | solution.py:374
  (21 shorter events, 0.1 us)
Async XLA Ops:
  7.2 59.6 %all-gather.3.cloned.1.call-start = ((), (), s32[]{:S(2)}) async-start(), calls=%async_computation.2 | async-start | bytes 1966080 | tf_op jit(solution)/shard_map/all_gather | solution.py:343
  8.6 39.8 %copy-start.7 = (s32[1,768,256]{1,2,0:T(8,128)}, s32[1,768,256]{1,2,0:T(8,128)S(1)}, u32[]{:S(2)}) copy-start(s32[1,768,256]{1,2,0:T(8,128)S(1)} %copy.13) | copy-start | bytes 2359300
  9.3 1.0 copy-start.3
  10.3 0.9 copy-start.5
  41.7 1.3 copy-start
  43.0 5.5 %copy-start.9 = (bf16[1,512]{1,0:T(2,128)(2,1)S(1)}, bf16[1,512]{1,0:T(2,128)(2,1)}, u32[]{:S(2)}) copy-start(bf16[1,512]{1,0:T(2,128)(2,1)} %param.15) | copy-start | bytes 3076
  43.0 7.0 %copy-start.10 = (s32[256]{0:T(256)S(1)}, s32[256]{0:T(256)}, u32[]{:S(2)}) copy-start(s32[256]{0:T(256)} %param.10) | copy-start | bytes 3076
  48.4 142.8 %reduce-scatter.2.cloned.1.call-start = ((), (), s32[]{:S(2)}) async-start(), calls=%async_computation.1 | async-start | bytes 1966080 | tf_op jit(solution)/shard_map/reduce_scatter | solution.py:372
  71.1 1.2 copy-start.6
  85.5 3.3 %copy-start.4 = (bf16[1,512,256]{2,1,0:T(8,128)(2,1)S(1)}, bf16[1,512,256]{2,1,0:T(8,128)(2,1)}, u32[]{:S(2)}) copy-start(bf16[1,512,256]{2,1,0:T(8,128)(2,1)} %param.9) | copy-start | bytes 786436
  142.6 1.3 copy-start.2
  170.0 21.2 %copy-start.1 = (bf16[8,512,256]{2,1,0:T(8,128)(2,1)S(1)}, bf16[8,512,256]{2,1,0:T(8,128)(2,1)}, u32[]{:S(2)}) copy-start(bf16[8,512,256]{2,1,0:T(8,128)(2,1)} %copy-done) | copy-start | bytes 6291460
  170.0 21.2 %copy-start.8 = (s32[1,768,256]{1,2,0:T(8,128)S(1)}, s32[1,768,256]{1,2,0:T(8,128)}, u32[]{:S(2)}) copy-start(s32[1,768,256]{1,2,0:T(8,128)} %copy-done.7) | copy-start | bytes 2359300
Sparse Core Ops, SparseCore 0:
  48.5 18.2 all-gather.2
  162.5 28.6 reduce-scatter.1

commit v2 on v1

--- a/solution.py
+++ b/solution.py
@@ -34,7 +34,7 @@
     )
 
 
-def greet(at):
+def greet(at, more=0):
     barrier = pltpu.get_barrier_semaphore()
 
     def hello(lat):
@@ -45,7 +45,7 @@
     hello(at.partner)
     pl.when(at.has_up)(lambda: hello(at.me + 2))
     pl.when(at.has_down)(lambda: hello(at.me - 2))
-    peers = 1 + at.has_up.astype(jnp.int32) + at.has_down.astype(jnp.int32)
+    peers = 1 + more + at.has_up.astype(jnp.int32) + at.has_down.astype(jnp.int32)
     pl.semaphore_wait(barrier, peers)
 
 
@@ -92,13 +92,14 @@
             pl.when(at.has_down)(lambda: self.hop(1, d).start())
             self.hop(3, d).start()
 
-    def finish(self):
+    def finish(self, crossed=False):
         at = self.at
         for d in range(at.depth):
 
             @pl.when(at.z >= d)
             def _():
-                self.landing(2, d).wait_recv()
+                if not crossed:
+                    self.landing(2, d).wait_recv()
                 self.hop(2, d).wait_send()
                 if d < at.depth - 1:
                     pl.when(at.has_up)(lambda: self.hop(0, d).wait_send())
@@ -106,7 +107,8 @@
             @pl.when(at.z + d < at.depth)
             def _():
                 if d > 0:
-                    self.landing(3, d).wait_recv()
+                    if not crossed:
+                        self.landing(3, d).wait_recv()
                     self.hop(3, d).wait_send()
                 if d < at.depth - 1:
                     pl.when(at.has_down)(lambda: self.hop(1, d).wait_send())
@@ -265,7 +267,388 @@
                 along(False, d).wait_send()
 
 
+def flow(at, gathers, use):
+    use(at.me)
+
+    def cross(d):
+        @pl.when(at.z >= d)
+        def _():
+            for one in gathers:
+                one.landing(2, d).wait_recv()
+            use(at.partner - 2 * d)
+
+        if d:
+
+            @pl.when(at.z + d < at.depth)
+            def _():
+                for one in gathers:
+                    one.landing(3, d).wait_recv()
+                use(at.partner + 2 * d)
+
+    for d in range(1, at.depth):
+        for one in gathers:
+            one.step(d)
+        pl.when(at.z >= d)(lambda: use(at.me - 2 * d))
+        pl.when(at.z + d < at.depth)(lambda: use(at.me + 2 * d))
+        cross(d - 1)
+    cross(at.depth - 1)
+    for one in gathers:
+        one.finish(crossed=True)
+
+
+def to_layer(src, dst, send_sem, recv_sem, layer):
+    return pltpu.make_async_remote_copy(
+        src_ref=src,
+        dst_ref=dst,
+        send_sem=send_sem,
+        recv_sem=recv_sem,
+        device_id={"layer": layer},
+        device_id_type=pl.DeviceIdType.MESH,
+    )
+
+
+def encode_kernel(
+    lat_count,
+    layer_count,
+    own,
+    wanted_ref,
+    weight,
+    bias_ref,
+    gate_ref,
+    whole,
+    stats,
+    acts,
+    stat,
+    blocks,
+    acc,
+    big_sems,
+    stat_sems,
+    local_sem,
+    block_sems,
+    layer_sems,
+):
+    at = Place(lat_count)
+    rows = own.shape[0]
+    pairs = layer_count // 2
+    layer = lax.axis_index("layer")
+    pair, core = layer // 2, layer % 2
+    mate = layer + 1 - 2 * core
+
+    def load(g):
+        return pltpu.make_async_copy(
+            weight.at[:, pl.ds(g * rows, rows)], blocks.at[g], block_sems.at[g]
+        )
+
+    for g in range(lat_count):
+        load(g).start()
+    barrier = pltpu.get_barrier_semaphore()
+    for k in range(1, pairs):
+        other = lax.rem(pair + k, pairs) * 2 + core
+        pl.semaphore_signal(
+            barrier, inc=1, device_id={"layer": other}, device_id_type=pl.DeviceIdType.MESH
+        )
+    pl.semaphore_signal(
+        barrier, inc=1, device_id={"layer": mate}, device_id_type=pl.DeviceIdType.MESH
+    )
+    greet(at, pairs)
+    big = Gather(at, own, whole, big_sems)
+    big.start()
+    keep = pltpu.make_async_copy(own, whole.at[at.me], local_sem)
+    keep.start()
+    wanted = wanted_ref[...].astype(F32)
+    centered = wanted - jnp.mean(wanted, axis=1, keepdims=True)
+    spread = jnp.sum(centered * centered, keepdims=True)
+    stat[...] = jnp.broadcast_to(spread, stat.shape)
+    stats[at.me] = stat[...]
+    small = Gather(at, stat, stats, stat_sems)
+    small.start()
+    acc[...] = jnp.broadcast_to(bias_ref[...], acc.shape)
+    for g in range(lat_count):
+        load(g).wait()
+    keep.wait()
+
+    def use(g):
+        acc[...] += jnp.dot(blocks[g], whole[g], preferred_element_type=F32)
+
+    flow(at, (big, small), use)
+    acts[layer] = (gate_ref[...].astype(F32) * acc[...]).astype(BF16)
+
+    def over(k):
+        ref = acts.at[layer]
+        return to_layer(
+            ref, ref, layer_sems.at[0, 0, k], layer_sems.at[1, 0, k], layer + 2 * k
+        )
+
+    def pass_on(k):
+        ref = acts.at[layer - 2 * k]
+        return to_layer(ref, ref, layer_sems.at[0, 1, k], layer_sems.at[1, 1, k], mate)
+
+    def landed(kind, k):
+        ref = acts.at[layer - 2 * k if kind == 0 else mate - 2 * k]
+        sem = layer_sems.at[1, kind, k]
+        return to_layer(ref, ref, layer_sems.at[0, kind, k], sem, mate)
+
+    for k in range(1, pairs):
+        pl.when(pair + k < pairs)(lambda: over(k).start())
+    pl.when(core == 0)(lambda: pass_on(0).start())
+    for k in range(1, pairs):
+
+        @pl.when(pair + k < pairs)
+        def _():
+            empty = jnp.zeros(acts.shape[1:], BF16)
+            acts[layer + 2 * k] = empty
+            acts[mate + 2 * k] = empty
+
+    @pl.when(core == 0)
+    def _():
+        acts[mate] = jnp.zeros(acts.shape[1:], BF16)
+
+    for k in range(1, pairs):
+
+        @pl.when(pair >= k)
+        def _():
+            landed(0, k).wait_recv()
+            pass_on(k).start()
+
+    pl.when(core == 1)(lambda: landed(1, 0).wait_recv())
+    for k in range(1, pairs):
+
+        @pl.when(pair >= k)
+        def _():
+            landed(1, k).wait_recv()
+            pass_on(k).wait_send()
+
+        pl.when(pair + k < pairs)(lambda: over(k).wait_send())
+    pl.when(core == 0)(lambda: pass_on(0).wait_send())
+
+
+def decode_kernel(
+    lat_count,
+    weight,
+    acts,
+    wanted_ref,
+    bias_ref,
+    kept_ref,
+    spread_ref,
+    whole,
+    stats,
+    rows_out,
+    blocks,
+    turned,
+    leaving_up,
+    leaving_down,
+    across_up,
+    across_down,
+    from_below,
+    from_above,
+    going_up,
+    going_down,
+    total,
+    grad,
+    stat,
+    acc,
+    block_sems,
+    across_sems,
+    line_sems,
+    big_sems,
+    stat_sems,
+):
+    at = Place(lat_count)
+    depth = at.depth
+    layer_count, lat_rows, tokens = acts.shape
+    width = blocks.shape[3]
+    layer = lax.axis_index("layer")
+
+    def load(g):
+        columns = pl.ds(pl.multiple_of(g * width, width), width)
+        return pltpu.make_async_copy(weight.at[:, :, columns], blocks.at[g], block_sems.at[g])
+
+    for cross in (True, False):
+        for d in range(depth - 1, -1, -1):
+            mine = at.partner if cross else at.me
+            pl.when(at.z + d < depth)(lambda: load(mine + 2 * d).start())
+            if d:
+                pl.when(at.z >= d)(lambda: load(mine - 2 * d).start())
+    greet(at)
+    for source in range(layer_count):
+        turned[source] = jnp.transpose(acts[source])
+
+    def part(g):
+        load(g).wait()
+        got = jnp.dot(turned[0], blocks[g, 0], preferred_element_type=F32)
+        for source in range(1, layer_count):
+            got += jnp.dot(turned[source], blocks[g, source], preferred_element_type=F32)
+        return got
+
+    def across(up, d):
+        row = 0 if up else 1
+        return send(
+            (leaving_up if up else leaving_down).at[d],
+            (across_up if up else across_down).at[d],
+            across_sems.at[0, row, d],
+            across_sems.at[1, row, d],
+            at.partner,
+        )
+
+    def along(up, d):
+        row = 0 if up else 1
+        return send(
+            (going_up if up else going_down).at[d],
+            (from_below if up else from_above).at[d - 1],
+            line_sems.at[0, row, d],
+            line_sems.at[1, row, d - 1],
+            at.me + 2 if up else at.me - 2,
+        )
+
+    def arrived(up, d):
+        row = 0 if up else 1
+        ref = (from_below if up else from_above).at[d]
+        send(ref, ref, line_sems.at[0, row, d], line_sems.at[1, row, d], at.partner).wait_recv()
+
+    def leave(up, d):
+        made = part(at.partner + 2 * d if up else at.partner - 2 * d)
+        (leaving_up if up else leaving_down)[d] = made.astype(BF16)
+        across(up, d).start()
+
+    for d in range(depth - 1, -1, -1):
+        pl.when(at.z + d < depth)(lambda: leave(True, d))
+        if d:
+            pl.when(at.z >= d)(lambda: leave(False, d))
+
+    def forward(up, d):
+        total[...] = part(at.me + 2 * d if up else at.me - 2 * d)
+        across(up, d).wait_recv()
+        total[...] += (across_up if up else across_down)[d].astype(F32)
+        if d < depth - 1:
+
+            @pl.when(at.has_down if up else at.has_up)
+            def _():
+                arrived(up, d)
+                total[...] += (from_below if up else from_above)[d].astype(F32)
+
+        (going_up if up else going_down)[d] = total[...].astype(BF16)
+        along(up, d).start()
+
+    for d in range(depth - 1, 0, -1):
+        pl.when(at.z + d < depth)(lambda: forward(True, d))
+        pl.when(at.z >= d)(lambda: forward(False, d))
+    total[...] = part(at.me) + bias_ref[...] - jnp.transpose(wanted_ref[...].astype(F32))
+    across(True, 0).wait_recv()
+    total[...] += across_up[0].astype(F32)
+
+    @pl.when(at.has_down)
+    def _():
+        arrived(True, 0)
+        total[...] += from_below[0].astype(F32)
+
+    @pl.when(at.has_up)
+    def _():
+        arrived(False, 0)
+        total[...] += from_above[0].astype(F32)
+
+    err = kept_ref[...] * total[...]
+    grad[...] = jnp.transpose(err / spread_ref[...]).astype(BF16)
+    big = Gather(at, grad, whole, big_sems)
+    big.start()
+    whole[at.me] = grad[...]
+    stat[...] = jnp.broadcast_to(jnp.sum(err * err, keepdims=True), stat.shape)
+    stats[at.me] = stat[...]
+    small = Gather(at, stat, stats, stat_sems)
+    small.start()
+    acc[...] = jnp.zeros_like(acc)
+
+    def use(g):
+        @pl.loop(0, layer_count)
+        def _(source):
+            acc[source] += jnp.dot(blocks[g, source], whole[g], preferred_element_type=F32)
+
+    flow(at, (big, small), use)
+    for source in range(layer_count):
+        wanted_here = (source <= layer).astype(F32)
+        rows_out[source] = (acc[source] * wanted_here).astype(BF16)
+    for d in range(depth - 1, -1, -1):
+
+        @pl.when(at.z + d < depth)
+        def _():
+            across(True, d).wait_send()
+            if d:
+                along(True, d).wait_send()
+
+        if d:
+
+            @pl.when(at.z >= d)
+            def _():
+                across(False, d).wait_send()
+                along(False, d).wait_send()
+
+
 VMEM = pl.BlockSpec(memory_space=pltpu.VMEM)
+HBM = pl.BlockSpec(memory_space=pl.ANY)
+
+
+def encode(inputs_local, wanted, weight, bias, gate, lat_count, layer_count):
+    rows, tokens = inputs_local.shape
+    lat_rows = weight.shape[0]
+    depth = lat_count // 2
+    return pl.pallas_call(
+        functools.partial(encode_kernel, lat_count, layer_count),
+        out_shape=(
+            jax.ShapeDtypeStruct((lat_count, rows, tokens), BF16),
+            jax.ShapeDtypeStruct((lat_count, 8, 128), F32),
+            jax.ShapeDtypeStruct((layer_count, lat_rows, tokens), BF16),
+        ),
+        in_specs=[VMEM, VMEM, HBM, VMEM, VMEM],
+        out_specs=(VMEM,) * 3,
+        scratch_shapes=[
+            pltpu.VMEM((8, 128), F32),
+            pltpu.VMEM((lat_count, lat_rows, rows), BF16),
+            pltpu.VMEM((lat_rows, tokens), F32),
+            pltpu.SemaphoreType.DMA((2, 4, depth + 1)),
+            pltpu.SemaphoreType.DMA((2, 4, depth + 1)),
+            pltpu.SemaphoreType.DMA,
+            pltpu.SemaphoreType.DMA((lat_count,)),
+            pltpu.SemaphoreType.DMA((2, 2, layer_count // 2)),
+        ],
+        compiler_params=pltpu.CompilerParams(
+            collective_id=2, has_side_effects=True, vmem_limit_bytes=40 << 20
+        ),
+    )(inputs_local, wanted, weight, bias, gate)
+
+
+def decode(weight, acts, wanted, bias, kept, spread, lat_count):
+    layer_count, lat_rows, tokens = acts.shape
+    rows = wanted.shape[0]
+    depth = lat_count // 2
+    slots = pltpu.VMEM((depth, tokens, rows), BF16)
+    return pl.pallas_call(
+        functools.partial(decode_kernel, lat_count),
+        out_shape=(
+            jax.ShapeDtypeStruct((lat_count, rows, tokens), BF16),
+            jax.ShapeDtypeStruct((lat_count, 8, 128), F32),
+            jax.ShapeDtypeStruct((layer_count, lat_rows, tokens), BF16),
+        ),
+        in_specs=[HBM] + [VMEM] * 5,
+        out_specs=(VMEM,) * 3,
+        scratch_shapes=[
+            pltpu.VMEM((lat_count, layer_count, lat_rows, rows), BF16),
+            pltpu.VMEM((layer_count, tokens, lat_rows), BF16),
+        ]
+        + [slots] * 8
+        + [
+            pltpu.VMEM((tokens, rows), F32),
+            pltpu.VMEM((rows, tokens), BF16),
+            pltpu.VMEM((8, 128), F32),
+            pltpu.VMEM((layer_count, lat_rows, tokens), F32),
+            pltpu.SemaphoreType.DMA((lat_count,)),
+            pltpu.SemaphoreType.DMA((2, 2, depth)),
+            pltpu.SemaphoreType.DMA((2, 2, depth)),
+            pltpu.SemaphoreType.DMA((2, 4, depth + 1)),
+            pltpu.SemaphoreType.DMA((2, 4, depth + 1)),
+        ],
+        compiler_params=pltpu.CompilerParams(
+            collective_id=3, has_side_effects=True, vmem_limit_bytes=58 << 20
+        ),
+    )(weight, acts, wanted, bias, kept, spread)
 
 
 def gather_inputs(inputs_local, wanted, lat_count):
@@ -332,39 +715,64 @@
     feature_count = weight_enc.shape[1]
     feature_rows, token_count = inputs_local.shape
     total_cells = feature_count * token_count
-    whole_inputs, target_stats = gather_inputs(inputs_local, wanted, lat_count)
-    whole_inputs = whole_inputs.reshape(feature_count, token_count)
-    spread = jnp.sum(target_stats[:, 0, 0]) / total_cells + EPSILON
-    preact = jnp.dot(weight_enc, whole_inputs, preferred_element_type=F32)
-    preact = preact + enc_bias[0].astype(F32)[:, None]
+    kept_tokens = (token_ids != 128000).astype(F32)
+    source_ids = jnp.arange(layer_count)
     gating = active_mask[0].astype(F32)
-    latents = (gating * preact).astype(BF16)
-    source_ids = jnp.arange(layer_count)
-    gathered = lax.all_gather(latents[None], "layer", axis=0, tiled=True)
-    acts_stack = jnp.where(
-        (source_ids <= layer_here)[:, None, None], gathered, jnp.zeros((), BF16)
-    )
-    stack_rows = acts_stack.reshape(layer_count * lat_rows, token_count)
     weight_rows = dec_weight[0].reshape(layer_count * lat_rows, feature_count)
-    kept_tokens = (token_ids != 128000).astype(F32)
-    parts = lax.dot_general(
-        weight_rows, stack_rows, (((0,), (0,)), ((), ())), preferred_element_type=F32
-    ).astype(BF16)
-    full_grad, err_stats = reduce_and_gather(
-        parts.reshape(lat_count, feature_rows, token_count),
-        wanted,
-        dec_bias[0].astype(F32)[:, None],
-        kept_tokens[None, :],
-        jnp.broadcast_to(spread, (1, token_count)),
-        lat_count,
-    )
+    fused = feature_rows % 128 == 0 and lat_rows % 128 == 0 and layer_count % 2 == 0
+    if fused:
+        whole_inputs, target_stats, acts_stack = encode(
+            inputs_local,
+            wanted,
+            weight_enc,
+            enc_bias[0].astype(F32)[:, None],
+            active_mask[0],
+            lat_count,
+            layer_count,
+        )
+        whole_inputs = whole_inputs.reshape(feature_count, token_count)
+        spread = jnp.sum(target_stats[:, 0, 0]) / total_cells + EPSILON
+        stack_rows = acts_stack.reshape(layer_count * lat_rows, token_count)
+        full_grad, err_stats, grad_rows = decode(
+            dec_weight[0],
+            acts_stack,
+            wanted,
+            dec_bias[0].astype(F32)[None, :],
+            kept_tokens[:, None],
+            jnp.broadcast_to(spread, (1, feature_rows)),
+            lat_count,
+        )
+    else:
+        whole_inputs, target_stats = gather_inputs(inputs_local, wanted, lat_count)
+        whole_inputs = whole_inputs.reshape(feature_count, token_count)
+        spread = jnp.sum(target_stats[:, 0, 0]) / total_cells + EPSILON
+        preact = jnp.dot(weight_enc, whole_inputs, preferred_element_type=F32)
+        preact = preact + enc_bias[0].astype(F32)[:, None]
+        latents = (gating * preact).astype(BF16)
+        gathered = lax.all_gather(latents[None], "layer", axis=0, tiled=True)
+        acts_stack = jnp.where(
+            (source_ids <= layer_here)[:, None, None], gathered, jnp.zeros((), BF16)
+        )
+        stack_rows = acts_stack.reshape(layer_count * lat_rows, token_count)
+        parts = lax.dot_general(
+            weight_rows, stack_rows, (((0,), (0,)), ((), ())), preferred_element_type=F32
+        ).astype(BF16)
+        full_grad, err_stats = reduce_and_gather(
+            parts.reshape(lat_count, feature_rows, token_count),
+            wanted,
+            dec_bias[0].astype(F32)[:, None],
+            kept_tokens[None, :],
+            jnp.broadcast_to(spread, (1, token_count)),
+            lat_count,
+        )
     full_grad = full_grad.reshape(feature_count, token_count)
     layer_loss = jnp.sum(err_stats[:, 0, 0]) / (2.0 * spread * total_cells)
     total_loss = lax.psum(layer_loss, "layer")
-    grad_rows = jnp.dot(weight_rows, full_grad, preferred_element_type=F32).reshape(
-        layer_count, lat_rows, token_count
-    )
-    grad_rows = (grad_rows * (source_ids <= layer_here).astype(F32)[:, None, None]).astype(BF16)
+    if not fused:
+        grad_rows = jnp.dot(weight_rows, full_grad, preferred_element_type=F32).reshape(
+            layer_count, lat_rows, token_count
+        )
+        grad_rows = (grad_rows * (source_ids <= layer_here).astype(F32)[:, None, None]).astype(BF16)
     dec_out = lax.dot_general(
         stack_rows, full_grad, (((1,), (1,)), ((), ())), preferred_element_type=F32
     )

time: 204 us -> 163 us (0.80)
  matrix products: 50.9 us -> 20.3 us
  waiting for transfers between devices: 23.5 us -> 4.64 us
  Pallas kernels: 84.2 us -> 97.1 us
  local copies, waits for them, and re-layouts: 18.9 us -> 9.88 us
  blocking collectives: 6.4 us -> 11.3 us
    dot_general x3 -> x0, matrix products: 30.8 us -> none  [the longest x1 13.2 us: on_device(): lax.dot_general(weight_rows, stack_rows, (((0,), (0,)), ((), ())), prefer...]
    all_gather x1 -> x0, waiting for transfers between devices: 16.8 us -> none  [on_device(): gathered = lax.all_gather(latents[None], 'layer', axis=0, tiled=True)]
    pallas_call x2, Pallas kernels: 84.2 us -> 97.1 us  [the longest x1 59.4 us: decode(): pl.pallas_call(functools.partial(decode_kernel, lat_count), out_shape=(ja...]
    psum x1, blocking collectives: 6.4 us -> 11.3 us  [on_device(): total_loss = lax.psum(layer_loss, 'layer')]
    all_gather x1 -> x0, local copies, waits for them, and re-layouts: 3.27 us -> none  [on_device(): gathered = lax.all_gather(latents[None], 'layer', axis=0, tiled=True)]
    convert_element_type x2 -> x1, local copies, waits for them, and re-layouts: 3.45 us -> 0.18 us  [on_device(): enc_bias[0].astype(F32)[:, None]]
    reshape x1 -> x0, local copies, waits for them, and re-layouts: 2.37 us -> none  [on_device(): jnp.dot(weight_rows, full_grad, preferred_element_type=F32)]
    dot_general x1 -> x0, local copies, waits for them, and re-layouts: 2.36 us -> none  [on_device(): jnp.dot(weight_rows, full_grad, preferred_element_type=F32)]
  transfers between devices with their start and end apart: 2 -> 1, of which waited for: 2 -> 1; matrix products, arithmetic and copies ran while one was open for 8% -> 10% of each run, Pallas kernels for 0% -> 0%
where the time goes in v2:
time: 163 us; the launch traced here: 162 us
  Pallas kernels  97.1 us (60%)
  matrix products  20.3 us (12%)
  between operations  15.4 us (9%)
  blocking collectives  11.3 us (7%)
  local copies, waits for them, and re-layouts  9.88 us (6%)
  waiting for transfers between devices  4.64 us (3%)
  other arithmetic  3.36 us (2%)
    pallas_call x1, Pallas kernels, decode(): pl.pallas_call(functools.partial(decode_kernel, lat_count), out_shape=(ja...  59.4 us
    pallas_call x1, Pallas kernels, encode(): pl.pallas_call(functools.partial(encode_kernel, lat_count, layer_count),...  37.7 us
    dot_general x1, matrix products, on_device(): lax.dot_general(stack_rows, full_grad, (((1,), (1,)), ((), ())), preferre...  14.1 us
    psum x1, blocking collectives, on_device(): total_loss = lax.psum(layer_loss, 'layer')  11.3 us
    unnamed x20, local copies, waits for them, and re-layouts  8.3 us
    dot_general x1, matrix products, on_device(): lax.dot_general(preact_grad, whole_inputs, (((1,), (1,)), ((), ())), pref...  6.29 us
    reduce_scatter x1, waiting for transfers between devices, on_device(): lax.psum_scatter(grad_rows, 'layer', scatter_dimension=0, tiled=True)[0]  4.62 us
  transfers between devices with their start and end apart: 1, of which 1 were waited for; matrix products, arithmetic and copies ran while one was open for 10% of the time, Pallas kernels for 0%

profile of v2, /device:TPU:0, one launch (start us, length us, event | category | flops | bytes accessed | tf_op | source)
XLA Modules:
  0.0 162.1 jit_solution(2823854042419162002)
XLA Ops:
  7.2 0.0 reduce-scatter.2.cloned.1.call-start
  7.2 0.7 bitcast_convert_fusion
  7.9 0.2 copy.11.bias_ref
  8.1 0.0 copy-start.2
  8.1 2.8 %copy-done.2 = bf16[1,768,4096]{2,1,0:T(8,128)(2,1)S(1)} copy-done((bf16[1,768,4096]{2,1,0:T(8,128)(2,1)S(1)}, bf16[1,768,4096]{2,1,0:T(8,128)(2,1)}, u32[]{:S(2)}) %copy-start.2) | copy-done | bytes 6291480
  10.9 0.0 copy-start.3
  10.9 1.1 copy-done.3
  12.0 0.0 copy-start.6
  12.0 0.9 copy-done.6
  13.0 0.0 copy-start.7
  13.0 0.9 copy-done.7
  13.9 0.0 copy-start.9
  13.9 37.7 %shard_map.103 = (bf16[8,512,256]{2,1,0:T(8,128)(2,1)S(1)}, f32[8,8,128]{2,1,0:T(8,128)S(1)}, bf16[4,768,256]{2,1,0:T(8,128)(2,1)S(1)}) custom-call(bf16[512,256]{1,0:T(8,128)(2,1)S(1)} %bitcast.27, bf16[512,256]{1,0:T(8,128)(2,1)S(1)} %bitcast.26, bf16[768,4096]{1,0:T(8,128)(2,1)S(1)} %bitcast.22, f32[768,1]{1,0:T(8,128)S(1)} %copy.11.bias_ref, ...), custom_call_target="tpu_custom_call" | custom-call | tf_op jit(solution)/shard_map/pallas_call | solution.py:593
  51.6 0.0 copy-start
  51.6 1.1 copy-done
  52.7 1.3 copy-done.5
  54.1 0.6 slice_reduce_fusion.1
  54.7 0.0 copy-done.9
  54.7 0.8 copy.12.kept_ref
  55.5 0.0 copy-done.8
  55.5 0.6 convert_element_type.41.bias_ref
  56.7 0.6 broadcast_in_dim.15.spread_ref
  57.3 59.4 %shard_map.104 = (bf16[8,512,256]{2,1,0:T(8,128)(2,1)}, f32[8,8,128]{2,1,0:T(8,128)}, bf16[4,768,256]{2,1,0:T(8,128)(2,1)}) custom-call(bf16[4,768,4096]{2,1,0:T(8,128)(2,1)} %bitcast.29, bf16[4,768,256]{2,1,0:T(8,128)(2,1)} %copy-done, bf16[512,256]{1,0:T(8,128)(2,1)} %bitcast.25, f32[1,512]{1,0:T(1,128)} %convert_element_type.41.bias_ref, ...), custom_call_target="tpu_custom_call" | custom-call | tf_op jit(solution)/shard_map/pallas_call | solution.py:623
  116.7 0.0 copy-start.1
  116.8 0.0 reduce-scatter.2.cloned.1.call-update
  116.8 1.5 slice_reduce_fusion
  118.9 11.3 %psum.7 = f32[]{:T(128)} all-reduce(f32[]{:T(128)S(6)} %div.7), channel_id=1, replica_groups=mesh['layer'=4,'lat'=8] {'layer'}, use_global_device_ids=true, to_apply=%region_3.0 | all-reduce | flops 1 | bytes 8 | tf_op jit(solution)/shard_map/psum | solution.py:770
  130.3 0.0 copy-done.1
  130.3 14.1 %convolution_convert_fusion = bf16[3072,4096]{1,0:T(8,128)(2,1)} fusion(bf16[3072,256]{1,0:T(8,128)(2,1)S(1)} %bitcast.21, bf16[4096,256]{1,0:T(8,128)(2,1)} %bitcast.30), kind=kOutput, calls=%fused_computation | convolution fusion | flops 6455033856 | bytes 28835840 | tf_op jit(solution)/shard_map/dot_general | solution.py:776
  144.3 4.6 %reduce-scatter.2.cloned.1.call-done = bf16[1,768,256]{2,1,0:T(8,128)(2,1)} async-done(((bf16[4,768,256]{2,1,0:T(8,128)(2,1)}), bf16[1,768,256]{2,1,0:T(8,128)(2,1)}) %reduce-scatter.2.cloned.1.call-update) | async-done | bytes 393232 | tf_op jit(solution)/shard_map/reduce_scatter | solution.py:780
  149.0 0.0 copy-done.4
  149.0 6.3 %fusion = bf16[1,768,4096]{2,1,0:T(8,128)(2,1)} fusion(bf16[4096,256]{1,0:T(8,128)(2,1)} %bitcast.24, bf16[1,768,256]{2,1,0:T(8,128)(2,1)} %reduce-scatter.2.cloned.1.call-done, s32[1,768,256]{2,1,0:T(8,128)S(1)} %copy-done.4), kind=kOutput, calls=%fused_computation.2 | convolution fusion | flops 1614544896 | bytes 9568256 | tf_op jit(solution)/shard_map/dot_general | solution.py:782
  (4 shorter events, 0.0 us)
Async XLA Ops:
  7.2 141.8 %reduce-scatter.2.cloned.1.call-start = ((), (), s32[]{:S(2)}) async-start(), calls=%async_computation.1 | async-start | bytes 1966080 | tf_op jit(solution)/shard_map/reduce_scatter | solution.py:780
  8.1 2.8 %copy-start.2 = (bf16[1,768,4096]{2,1,0:T(8,128)(2,1)S(1)}, bf16[1,768,4096]{2,1,0:T(8,128)(2,1)}, u32[]{:S(2)}) copy-start(bf16[1,768,4096]{2,1,0:T(8,128)(2,1)} %param.12) | copy-start | bytes 18874372
  10.9 1.1 copy-start.3
  12.0 0.9 copy-start.6
  13.0 0.9 copy-start.7
  13.9 40.8 %copy-start.9 = (s32[256]{0:T(256)S(1)}, s32[256]{0:T(256)}, u32[]{:S(2)}) copy-start(s32[256]{0:T(256)} %param.10) | copy-start | bytes 3076
  13.9 41.6 %copy-start.8 = (bf16[1,512]{1,0:T(2,128)(2,1)S(1)}, bf16[1,512]{1,0:T(2,128)(2,1)}, u32[]{:S(2)}) copy-start(bf16[1,512]{1,0:T(2,128)(2,1)} %param.15) | copy-start | bytes 3076
  51.6 1.1 copy-start
  52.7 1.3 copy-start.5
  116.7 13.5 %copy-start.1 = (bf16[4,768,256]{2,1,0:T(8,128)(2,1)S(1)}, bf16[4,768,256]{2,1,0:T(8,128)(2,1)}, u32[]{:S(2)}) copy-start(bf16[4,768,256]{2,1,0:T(8,128)(2,1)} %copy-done) | copy-start | bytes 4718596
  130.3 18.7 %copy-start.4 = (s32[1,768,256]{2,1,0:T(8,128)S(1)}, s32[1,768,256]{2,1,0:T(8,128)}, u32[]{:S(2)}) copy-start(s32[1,768,256]{2,1,0:T(8,128)} %param.11) | copy-start | bytes 2359300
Sparse Core Ops, SparseCore 0:
  116.9 32.0 reduce-scatter.1

commit v3 on v2

--- a/solution.py
+++ b/solution.py
@@ -319,11 +319,13 @@
     stats,
     acts,
     stat,
+    wanted_here,
+    gate_here,
     blocks,
     acc,
     big_sems,
     stat_sems,
-    local_sem,
+    local_sems,
     block_sems,
     layer_sems,
 ):
@@ -339,8 +341,12 @@
             weight.at[:, pl.ds(g * rows, rows)], blocks.at[g], block_sems.at[g]
         )
 
+    fetch = pltpu.make_async_copy(wanted_ref, wanted_here, local_sems.at[1])
+    fetch.start()
+    fetch_gate = pltpu.make_async_copy(gate_ref, gate_here, local_sems.at[2])
     for g in range(lat_count):
         load(g).start()
+    fetch_gate.start()
     barrier = pltpu.get_barrier_semaphore()
     for k in range(1, pairs):
         other = lax.rem(pair + k, pairs) * 2 + core
@@ -353,9 +359,10 @@
     greet(at, pairs)
     big = Gather(at, own, whole, big_sems)
     big.start()
-    keep = pltpu.make_async_copy(own, whole.at[at.me], local_sem)
+    keep = pltpu.make_async_copy(own, whole.at[at.me], local_sems.at[0])
     keep.start()
-    wanted = wanted_ref[...].astype(F32)
+    fetch.wait()
+    wanted = wanted_here[...].astype(F32)
     centered = wanted - jnp.mean(wanted, axis=1, keepdims=True)
     spread = jnp.sum(centered * centered, keepdims=True)
     stat[...] = jnp.broadcast_to(spread, stat.shape)
@@ -371,7 +378,8 @@
         acc[...] += jnp.dot(blocks[g], whole[g], preferred_element_type=F32)
 
     flow(at, (big, small), use)
-    acts[layer] = (gate_ref[...].astype(F32) * acc[...]).astype(BF16)
+    fetch_gate.wait()
+    acts[layer] = (gate_here[...].astype(F32) * acc[...]).astype(BF16)
 
     def over(k):
         ref = acts.at[layer]
@@ -428,11 +436,17 @@
     acts,
     wanted_ref,
     bias_ref,
-    kept_ref,
-    spread_ref,
+    ids_ref,
+    spread_stats,
     whole,
+    loss,
+    own_term,
+    terms,
+    wanted_here,
     stats,
-    rows_out,
+    losses,
+    giving,
+    given,
     blocks,
     turned,
     leaving_up,
@@ -447,6 +461,9 @@
     grad,
     stat,
     acc,
+    wanted_sem,
+    mate_sems,
+    loss_sems,
     block_sems,
     across_sems,
     line_sems,
@@ -458,6 +475,10 @@
     layer_count, lat_rows, tokens = acts.shape
     width = blocks.shape[3]
     layer = lax.axis_index("layer")
+    pairs = layer_count // 2
+    pair, core = layer // 2, layer % 2
+    mate = layer + 1 - 2 * core
+    cells = lat_count * width * tokens
 
     def load(g):
         columns = pl.ds(pl.multiple_of(g * width, width), width)
@@ -469,7 +490,15 @@
             pl.when(at.z + d < depth)(lambda: load(mine + 2 * d).start())
             if d:
                 pl.when(at.z >= d)(lambda: load(mine - 2 * d).start())
-    greet(at)
+    fetch = pltpu.make_async_copy(wanted_ref, wanted_here, wanted_sem)
+    fetch.start()
+    barrier = pltpu.get_barrier_semaphore()
+    for k in range(1, layer_count):
+        other = lax.rem(layer + k, layer_count)
+        pl.semaphore_signal(
+            barrier, inc=1, device_id={"layer": other}, device_id_type=pl.DeviceIdType.MESH
+        )
+    greet(at, layer_count - 1)
     for source in range(layer_count):
         turned[source] = jnp.transpose(acts[source])
 
@@ -532,7 +561,9 @@
     for d in range(depth - 1, 0, -1):
         pl.when(at.z + d < depth)(lambda: forward(True, d))
         pl.when(at.z >= d)(lambda: forward(False, d))
-    total[...] = part(at.me) + bias_ref[...] - jnp.transpose(wanted_ref[...].astype(F32))
+    fetch.wait()
+    goal = jnp.transpose(wanted_here[...].astype(F32))
+    total[...] = part(at.me) + bias_ref[...].astype(F32) - goal
     across(True, 0).wait_recv()
     total[...] += across_up[0].astype(F32)
 
@@ -546,8 +577,9 @@
         arrived(False, 0)
         total[...] += from_above[0].astype(F32)
 
-    err = kept_ref[...] * total[...]
-    grad[...] = jnp.transpose(err / spread_ref[...]).astype(BF16)
+    err = (ids_ref[...] != 128000).astype(F32) * jnp.transpose(total[...])
+    spread = jnp.sum(spread_stats[...], axis=0) / cells + EPSILON
+    grad[...] = (err / jnp.max(spread, keepdims=True)).astype(BF16)
     big = Gather(at, grad, whole, big_sems)
     big.start()
     whole[at.me] = grad[...]
@@ -563,9 +595,55 @@
             acc[source] += jnp.dot(blocks[g, source], whole[g], preferred_element_type=F32)
 
     flow(at, (big, small), use)
-    for source in range(layer_count):
-        wanted_here = (source <= layer).astype(F32)
-        rows_out[source] = (acc[source] * wanted_here).astype(BF16)
+    losses[layer] = jnp.sum(stats[...], axis=0) / (2.0 * spread * cells)
+
+    def tell(k):
+        ref = losses.at[layer]
+        other = lax.rem(layer + k, layer_count)
+        return to_layer(ref, ref, loss_sems.at[0, k], loss_sems.at[1, k], other)
+
+    def told(k):
+        other = lax.rem(layer - k + layer_count, layer_count)
+        ref = losses.at[other]
+        return to_layer(ref, ref, loss_sems.at[0, k], loss_sems.at[1, k], other)
+
+    def give(k):
+        return to_layer(
+            giving.at[k], given.at[k], mate_sems.at[0, k], mate_sems.at[1, k], mate
+        )
+
+    def hand(k):
+        giving[k] = acc[mate - 2 * k].astype(BF16)
+        give(k).start()
+
+    for k in range(pairs - 1, 0, -1):
+        pl.when(pair >= k)(lambda: hand(k))
+    pl.when(core == 1)(lambda: hand(0))
+    for k in range(1, layer_count):
+        tell(k).start()
+    own_term[...] = acc[layer]
+    for k in range(pairs - 1, 0, -1):
+
+        @pl.when(pair >= k)
+        def _():
+            give(k).wait_recv()
+            terms[k - 1] = (acc[layer - 2 * k] + given[k].astype(F32)).astype(BF16)
+            give(k).wait_send()
+
+        @pl.when(pair < k)
+        def _():
+            terms[k - 1] = jnp.zeros(terms.shape[1:], BF16)
+
+    @pl.when(core == 0)
+    def _():
+        give(0).wait_recv()
+        own_term[...] += given[0].astype(F32)
+
+    pl.when(core == 1)(lambda: give(0).wait_send())
+    for k in range(1, layer_count):
+        told(k).wait_recv()
+        tell(k).wait_send()
+    loss[...] = jnp.sum(losses[...], axis=0)
     for d in range(depth - 1, -1, -1):
 
         @pl.when(at.z + d < depth)
@@ -583,7 +661,7 @@
 
 
 VMEM = pl.BlockSpec(memory_space=pltpu.VMEM)
-HBM = pl.BlockSpec(memory_space=pl.ANY)
+HBM = pl.BlockSpec(memory_space=pltpu.HBM)
 
 
 def encode(inputs_local, wanted, weight, bias, gate, lat_count, layer_count):
@@ -597,39 +675,48 @@
             jax.ShapeDtypeStruct((lat_count, 8, 128), F32),
             jax.ShapeDtypeStruct((layer_count, lat_rows, tokens), BF16),
         ),
-        in_specs=[VMEM, VMEM, HBM, VMEM, VMEM],
+        in_specs=[HBM, HBM, HBM, VMEM, HBM],
         out_specs=(VMEM,) * 3,
         scratch_shapes=[
             pltpu.VMEM((8, 128), F32),
+            pltpu.VMEM((rows, tokens), BF16),
+            pltpu.VMEM((lat_rows, tokens), jnp.int32),
             pltpu.VMEM((lat_count, lat_rows, rows), BF16),
             pltpu.VMEM((lat_rows, tokens), F32),
             pltpu.SemaphoreType.DMA((2, 4, depth + 1)),
             pltpu.SemaphoreType.DMA((2, 4, depth + 1)),
-            pltpu.SemaphoreType.DMA,
+            pltpu.SemaphoreType.DMA((3,)),
             pltpu.SemaphoreType.DMA((lat_count,)),
             pltpu.SemaphoreType.DMA((2, 2, layer_count // 2)),
         ],
         compiler_params=pltpu.CompilerParams(
-            collective_id=2, has_side_effects=True, vmem_limit_bytes=40 << 20
+            collective_id=2, has_side_effects=True, vmem_limit_bytes=58 << 20
         ),
     )(inputs_local, wanted, weight, bias, gate)
 
 
-def decode(weight, acts, wanted, bias, kept, spread, lat_count):
+def decode(weight, acts, wanted, bias, ids, spread_stats, lat_count):
     layer_count, lat_rows, tokens = acts.shape
     rows = wanted.shape[0]
     depth = lat_count // 2
+    pairs = layer_count // 2
     slots = pltpu.VMEM((depth, tokens, rows), BF16)
     return pl.pallas_call(
         functools.partial(decode_kernel, lat_count),
         out_shape=(
             jax.ShapeDtypeStruct((lat_count, rows, tokens), BF16),
-            jax.ShapeDtypeStruct((lat_count, 8, 128), F32),
-            jax.ShapeDtypeStruct((layer_count, lat_rows, tokens), BF16),
+            jax.ShapeDtypeStruct((8, 128), F32),
+            jax.ShapeDtypeStruct((lat_rows, tokens), F32),
+            jax.ShapeDtypeStruct((pairs - 1, lat_rows, tokens), BF16),
         ),
-        in_specs=[HBM] + [VMEM] * 5,
-        out_specs=(VMEM,) * 3,
+        in_specs=[HBM, VMEM, HBM] + [VMEM] * 3,
+        out_specs=(VMEM,) * 4,
         scratch_shapes=[
+            pltpu.VMEM((rows, tokens), BF16),
+            pltpu.VMEM((lat_count, 8, 128), F32),
+            pltpu.VMEM((layer_count, 8, 128), F32),
+            pltpu.VMEM((pairs, lat_rows, tokens), BF16),
+            pltpu.VMEM((pairs, lat_rows, tokens), BF16),
             pltpu.VMEM((lat_count, layer_count, lat_rows, rows), BF16),
             pltpu.VMEM((layer_count, tokens, lat_rows), BF16),
         ]
@@ -639,6 +726,9 @@
             pltpu.VMEM((rows, tokens), BF16),
             pltpu.VMEM((8, 128), F32),
             pltpu.VMEM((layer_count, lat_rows, tokens), F32),
+            pltpu.SemaphoreType.DMA,
+            pltpu.SemaphoreType.DMA((2, pairs)),
+            pltpu.SemaphoreType.DMA((2, layer_count)),
             pltpu.SemaphoreType.DMA((lat_count,)),
             pltpu.SemaphoreType.DMA((2, 2, depth)),
             pltpu.SemaphoreType.DMA((2, 2, depth)),
@@ -648,7 +738,7 @@
         compiler_params=pltpu.CompilerParams(
             collective_id=3, has_side_effects=True, vmem_limit_bytes=58 << 20
         ),
-    )(weight, acts, wanted, bias, kept, spread)
+    )(weight, acts, wanted, bias, ids, spread_stats)
 
 
 def gather_inputs(inputs_local, wanted, lat_count):
@@ -719,7 +809,9 @@
     source_ids = jnp.arange(layer_count)
     gating = active_mask[0].astype(F32)
     weight_rows = dec_weight[0].reshape(layer_count * lat_rows, feature_count)
-    fused = feature_rows % 128 == 0 and lat_rows % 128 == 0 and layer_count % 2 == 0
+    pairs = layer_count // 2
+    fused = feature_rows % 128 == 0 and lat_rows % 128 == 0 and layer_count == 2 * pairs
+    fused = fused and pairs > 1
     if fused:
         whole_inputs, target_stats, acts_stack = encode(
             inputs_local,
@@ -731,15 +823,14 @@
             layer_count,
         )
         whole_inputs = whole_inputs.reshape(feature_count, token_count)
-        spread = jnp.sum(target_stats[:, 0, 0]) / total_cells + EPSILON
         stack_rows = acts_stack.reshape(layer_count * lat_rows, token_count)
-        full_grad, err_stats, grad_rows = decode(
+        full_grad, loss_tile, latent_grad, terms = decode(
             dec_weight[0],
             acts_stack,
             wanted,
-            dec_bias[0].astype(F32)[None, :],
-            kept_tokens[:, None],
-            jnp.broadcast_to(spread, (1, feature_rows)),
+            dec_bias,
+            token_ids[None, :],
+            target_stats,
             lat_count,
         )
     else:
@@ -766,9 +857,19 @@
             lat_count,
         )
     full_grad = full_grad.reshape(feature_count, token_count)
-    layer_loss = jnp.sum(err_stats[:, 0, 0]) / (2.0 * spread * total_cells)
-    total_loss = lax.psum(layer_loss, "layer")
-    if not fused:
+    if fused:
+        total_loss = loss_tile[0, 0]
+        moved = [
+            lax.ppermute(
+                terms[k - 1],
+                "layer",
+                [(d, d - 2 * k) for d in range(2 * k, layer_count)],
+            )
+            for k in range(1, pairs)
+        ]
+    else:
+        layer_loss = jnp.sum(err_stats[:, 0, 0]) / (2.0 * spread * total_cells)
+        total_loss = lax.psum(layer_loss, "layer")
         grad_rows = jnp.dot(weight_rows, full_grad, preferred_element_type=F32).reshape(
             layer_count, lat_rows, token_count
         )
@@ -777,7 +878,11 @@
         stack_rows, full_grad, (((1,), (1,)), ((), ())), preferred_element_type=F32
     )
     dec_out = dec_out.astype(BF16).reshape(1, layer_count, lat_rows, feature_count)
-    latent_grad = lax.psum_scatter(grad_rows, "layer", scatter_dimension=0, tiled=True)[0]
+    if fused:
+        for came in moved:
+            latent_grad = latent_grad + came.astype(F32)
+    else:
+        latent_grad = lax.psum_scatter(grad_rows, "layer", scatter_dimension=0, tiled=True)[0]
     preact_grad = (gating * latent_grad.astype(F32)).astype(BF16)
     enc_out = lax.dot_general(
         preact_grad, whole_inputs, (((1,), (1,)), ((), ())), preferred_element_type=F32

time: 163 us -> 133 us (0.82)
  between operations: 15.4 us -> 0.69 us
  blocking collectives: 11.3 us -> 0 us
  Pallas kernels: 97.1 us -> 108 us
  local copies, waits for them, and re-layouts: 9.88 us -> 2.15 us
  waiting for transfers between devices: 4.64 us -> 0.01 us
  other arithmetic: 3.36 us -> 0.69 us
    psum x1 -> x0, blocking collectives: 11.3 us -> none  [on_device(): total_loss = lax.psum(layer_loss, 'layer')]
    unnamed x20 -> x6, local copies, waits for them, and re-layouts: 8.3 us -> 0.01 us
    pallas_call x1, Pallas kernels: 59.4 us -> 67.7 us  [decode(): pl.pallas_call(functools.partial(decode_kernel, lat_count), out_shape=(ja...]
    reduce_scatter x1 -> x0, waiting for transfers between devices: 4.62 us -> none  [on_device(): lax.psum_scatter(grad_rows, 'layer', scatter_dimension=0, tiled=True)[0]]
    pallas_call x1, Pallas kernels: 37.7 us -> 39.9 us  [encode(): pl.pallas_call(functools.partial(encode_kernel, lat_count, layer_count),...]
    reduce_sum x2 -> x0, other arithmetic: 2.09 us -> none  [the longest x1 1.49 us: on_device(): layer_loss = jnp.sum(err_stats[:, 0, 0]) / (2.0 * spread * total_cells)]
  transfers between devices with their start and end apart: 1 -> 1, of which waited for: 1 -> 0; matrix products, arithmetic and copies ran while one was open for 10% -> 12% of each run, Pallas kernels for 0% -> 0%
where the time goes in v3:
time: 133 us
  Pallas kernels  108 us (81%)
  matrix products  20.3 us (15%)
  local copies, waits for them, and re-layouts  2.15 us (2%)
  starting transfers between devices  1.51 us (1%)
    pallas_call x1, Pallas kernels, decode(): pl.pallas_call(functools.partial(decode_kernel, lat_count), out_shape=(ja...  67.7 us
    pallas_call x1, Pallas kernels, encode(): pl.pallas_call(functools.partial(encode_kernel, lat_count, layer_count),...  39.9 us
    dot_general x1, matrix products, on_device(): lax.dot_general(stack_rows, full_grad, (((1,), (1,)), ((), ())), preferre...  14.1 us
    dot_general x1, matrix products, on_device(): lax.dot_general(preact_grad, whole_inputs, (((1,), (1,)), ((), ())), pref...  6.14 us
  transfers between devices with their start and end apart: 1, of which 0 were waited for; matrix products, arithmetic and copies ran while one was open for 12% of the time, Pallas kernels for 0%

profile of v3, /device:TPU:0, one launch (start us, length us, event | category | flops | bytes accessed | tf_op | source)
XLA Modules:
  0.0 132.8 jit_solution(12295524667493878567)
XLA Ops:
  0.6 0.7 bitcast_convert_fusion
  1.3 0.9 copy.11.bias_ref
  2.3 39.9 %shard_map.103 = (bf16[8,512,256]{2,1,0:T(8,128)(2,1)}, f32[8,8,128]{2,1,0:T(8,128)}, bf16[4,768,256]{2,1,0:T(8,128)(2,1)}) custom-call(bf16[512,256]{1,0:T(8,128)(2,1)} %bitcast.33, bf16[512,256]{1,0:T(8,128)(2,1)} %bitcast.31, bf16[768,4096]{1,0:T(8,128)(2,1)} %bitcast.27, f32[768,1]{1,0:T(8,128)} %copy.11.bias_ref, s32[768,256]{1,0:T(8,128)} %bitcast.28), custom_call_target="tpu_custom_call" | custom-call | tf_op jit(solution)/shard_map/pallas_call | solution.py:671
  42.1 0.0 copy-start
  42.2 67.7 %shard_map.104 = (bf16[8,512,256]{2,1,0:T(8,128)(2,1)}, f32[8,128]{1,0:T(8,128)}, f32[768,256]{1,0:T(8,128)}, bf16[1,768,256]{2,1,0:T(8,128)(2,1)}) custom-call(bf16[4,768,4096]{2,1,0:T(8,128)(2,1)} %bitcast.25, bf16[4,768,256]{2,1,0:T(8,128)(2,1)} %get-tuple-element.10.acts, bf16[512,256]{1,0:T(8,128)(2,1)} %bitcast.32, bf16[1,512]{1,0:T(2,128)(2,1)} %bias_ref.1, ...), custom_call_target="tpu_custom_call" | custom-call | tf_op jit(solution)/shard_map/pallas_call | solution.py:704
  109.8 1.5 %collective-permute-start = (bf16[768,256]{1,0:T(8,128)(2,1)}, bf16[768,256]{1,0:T(8,128)(2,1)S(1)}, u32[]{:S(2)}, u32[]{:S(2)}) collective-permute-start(bf16[768,256]{1,0:T(8,128)(2,1)} %bitcast.35), channel_id=1, source_target_pairs={{16,0},{24,8},{17,1},{25,9},{18,2},{26,10},{19,3},{27,11},{20,4},{... | collective-permute-start | bytes 1179656 | tf_op jit(solution)/shard_map/ppermute | solution.py:863
  111.3 0.0 copy-done
  111.3 0.0 copy-start.1
  111.4 0.0 copy-start.2
  111.4 14.1 %convolution_convert_fusion = bf16[3072,4096]{1,0:T(8,128)(2,1)} fusion(bf16[3072,256]{1,0:T(8,128)(2,1)S(1)} %bitcast.26, bf16[4096,256]{1,0:T(8,128)(2,1)} %bitcast.30), kind=kOutput, calls=%fused_computation | convolution fusion | flops 6455033856 | bytes 28835840 | tf_op jit(solution)/shard_map/dot_general | solution.py:877
  125.5 1.2 slice.3
  126.7 0.0 collective-permute-done
  126.7 0.0 copy-done.1
  126.7 0.0 copy-done.2
  126.7 6.1 %fusion = bf16[1,768,4096]{2,1,0:T(8,128)(2,1)} fusion(bf16[4096,256]{1,0:T(8,128)(2,1)} %bitcast.29, f32[768,256]{1,0:T(8,128)S(1)} %copy-done.2, bf16[768,256]{1,0:T(8,128)(2,1)S(1)} %collective-permute-done, s32[1,768,256]{2,1,0:T(8,128)S(1)} %copy-done.1), kind=kOutput, calls=%fused_computation.2 | convolution fusion | flops 1614741504 | bytes 10354688 | tf_op jit(solution)/shard_map/dot_general | solution.py:887
Async XLA Ops:
  42.1 69.2 %copy-start = (bf16[4,768,256]{2,1,0:T(8,128)(2,1)S(1)}, bf16[4,768,256]{2,1,0:T(8,128)(2,1)}, u32[]{:S(2)}) copy-start(bf16[4,768,256]{2,1,0:T(8,128)(2,1)} %get-tuple-element.10.acts) | copy-start | bytes 4718596
  109.8 16.9 %collective-permute-start = (bf16[768,256]{1,0:T(8,128)(2,1)}, bf16[768,256]{1,0:T(8,128)(2,1)S(1)}, u32[]{:S(2)}, u32[]{:S(2)}) collective-permute-start(bf16[768,256]{1,0:T(8,128)(2,1)} %bitcast.35), channel_id=1, source_target_pairs={{16,0},{24,8},{17,1},{25,9},{18,2},{26,10},{19,3},{27,11},{20,4},{... | collective-permute-start | bytes 1179656 | tf_op jit(solution)/shard_map/ppermute | solution.py:863
  111.3 15.3 %copy-start.1 = (s32[1,768,256]{2,1,0:T(8,128)S(1)}, s32[1,768,256]{2,1,0:T(8,128)}, u32[]{:S(2)}) copy-start(s32[1,768,256]{2,1,0:T(8,128)} %param.11) | copy-start | bytes 2359300
  111.4 15.3 %copy-start.2 = (f32[768,256]{1,0:T(8,128)S(1)}, f32[768,256]{1,0:T(8,128)}, u32[]{:S(2)}) copy-start(f32[768,256]{1,0:T(8,128)} %get-tuple-element.12) | copy-start | bytes 2359300
